TPU v7x, 32 devices: a whole 2x2x4 slice. The times are simulated.
32 devices in a mesh: groups: 2 (over y), tensor: 4 (over z), store: 4 (over x, core).
Axes of the slice: x: 2, y: 2, z: 4, core: 2. Of those that a mesh axis runs over, the one named last changes fastest.
Arguments:
- tokens: bfloat16 [4096, 8192], P(('groups', 'store', 'tensor')), parts along dimension 0, may hold values from -32 to 32
- query_weight: bfloat16 [8192, 8192], P(None, 'tensor'), may hold values from -0.0625 to 0.0625
- key_value_weight: bfloat16 [8192, 2048], P(None, 'tensor'), may hold values from -0.0625 to 0.0625
- adapter_down_maps: bfloat16 [32, 128, 8192], P('store', None, 'tensor'), may hold values from -0.0625 to 0.0625
- adapter_up_query: bfloat16 [32, 64, 8192], P('store', None, 'tensor'), may hold values from -0.375 to 0.375
- adapter_up_key_value: bfloat16 [32, 64, 2048], P('store', None, 'tensor'), may hold values from -0.375 to 0.375
- adapter_row_table: int32 [64], P('groups'), parts along dimension 0, may hold values from 0 to 31, as said below
- request_adapter_ids: int32 [8, 4], P('groups'), parts along dimension 0, may hold values from 0 to 31, as said below
- token_request_ids: int32 [8, 512], P(('groups', 'store')), parts along dimension 0, may hold values from 0 to 3, never falling along the last dimension, each value on 1 to 256 neighbouring positions
Outputs:
- attention: bfloat16 [4096, 8192], P(('groups', 'store'), 'tensor'), parts along dimension 0
There are 2 independent parts, one for each index of `groups`. A program takes and returns all parts, laid end to end along the dimension named above; an argument that names none is the same for every part. Nothing has to cross between parts.
Inputs may be any that keep to these rules, and one draw needn't show every extreme that they name: A permutation: adapter a lies in row adapter_row_table[a] of the adapter arrays, on store index adapter_row_table[a] // 8. `request_adapter_ids`: the 4 requests of one store batch use adapters held on 4 different store indices. `token_request_ids`: requests are contiguous runs of a store batch, each of 1 to 256 tokens.
All inputs are finite; a program needn't handle non-finite values.
Results may differ from a plain program's by a relative error of at most 0.012.
The roundings to bfloat16 on the way count: a program that leaves them out, or rounds other values in their place, can miss the bound.
Values may be sent and summed in bfloat16 or wider, within the bound.
A program may use at most 128 MiB of HBM per device.

v0:
```python
import math
import jax
import jax.numpy as jnp
from jax import lax
from jax.sharding import PartitionSpec as P

MODEL_WIDTH = 8192
QUERY_HEADS = 64
KEY_VALUE_HEADS = 8
HEAD_SIZE = 128
ADAPTER_RANK = 64
STORE_REQUESTS = 4
TOK_ST = 512
adapter_scale = 2.0
rope_theta = 500000.0


def from_partner(shard, axis, bit):
    return lax.ppermute(shard, axis, [(i, i ^ 1 << bit) for i in range(lax.axis_size(axis))])


def token_positions(segment_row):
    members = segment_row[:, None] == jnp.arange(STORE_REQUESTS, dtype=jnp.int32)[None, :]
    counts = jnp.sum(members.astype(jnp.int32), axis=0)
    starts = jnp.cumsum(counts) - counts
    first_index = jnp.sum(jnp.where(members, starts[None, :], 0), axis=1)
    return jnp.arange(segment_row.shape[0], dtype=jnp.int32) - first_index


def rotary(heads_values, positions):
    half_size = heads_values.shape[-1] // 2
    exponent = jnp.arange(half_size, dtype=jnp.float32) * (2.0 / heads_values.shape[-1])
    frequency = jnp.exp(-exponent * math.log(rope_theta))
    angles = positions.astype(jnp.float32)[:, None] * frequency[None, :]
    cosine = jnp.cos(angles)[:, None, :]
    sine = jnp.sin(angles)[:, None, :]
    lower = heads_values[..., :half_size]
    upper = heads_values[..., half_size:]
    return jnp.concatenate([lower * cosine - upper * sine, upper * cosine + lower * sine], axis=-1)


def select_rows(selector, stack):
    flat = stack.reshape(stack.shape[0], -1)
    picked = jnp.dot(selector, flat, preferred_element_type=jnp.float32)
    return picked.reshape(selector.shape[:-1] + stack.shape[1:])


def on_device(
    tokens,
    query_weight,
    key_value_weight,
    adapter_down_maps,
    adapter_up_query,
    adapter_up_key_value,
    adapter_row_table,
    request_adapter_ids,
    token_request_ids,
):
    tensor_rank = lax.axis_index("tensor")
    store_rank = lax.axis_index("store")
    tensor_count = lax.axis_size("tensor")
    store_count = lax.axis_size("store")
    position_count = adapter_down_maps.shape[0]
    adapter_total = adapter_row_table.shape[0]
    lookup = (
        request_adapter_ids[:, :, None] == jnp.arange(adapter_total, dtype=jnp.int32)[None, None, :]
    ).astype(jnp.int32)
    slot_table = jnp.sum(lookup * adapter_row_table[None, None, :], axis=2)
    my_slots = lax.dynamic_index_in_dim(slot_table, store_rank, 0, keepdims=False)
    local_slots = store_rank * position_count + jnp.arange(position_count, dtype=jnp.int32)
    serving = jnp.sum(
        (slot_table[:, :, None] == local_slots[None, None, :]).astype(jnp.int32), axis=1
    ).astype(jnp.bfloat16)
    out_down = select_rows(serving, adapter_down_maps).astype(jnp.bfloat16)
    out_query = select_rows(serving, adapter_up_query).astype(jnp.bfloat16)
    out_keyval = select_rows(serving, adapter_up_key_value).astype(jnp.bfloat16)
    got_down, got_query, got_keyval = (
        lax.all_to_all(out_down, "store", split_axis=0, concat_axis=0, tiled=True),
        lax.all_to_all(out_query, "store", split_axis=0, concat_axis=0, tiled=True),
        lax.all_to_all(out_keyval, "store", split_axis=0, concat_axis=0, tiled=True),
    )
    holder_pick = (
        (my_slots // position_count)[:, None] == jnp.arange(store_count, dtype=jnp.int32)[None, :]
    ).astype(jnp.bfloat16)
    down_blocks = select_rows(holder_pick, got_down).astype(jnp.bfloat16)
    up_query_blocks = select_rows(holder_pick, got_query).astype(jnp.bfloat16)
    up_keyval_blocks = select_rows(holder_pick, got_keyval).astype(jnp.bfloat16)
    segment_row = token_request_ids[0]
    members = segment_row[:, None] == jnp.arange(STORE_REQUESTS, dtype=jnp.int32)[None, :]
    member_float = members.astype(jnp.float32)
    member_half = members.astype(jnp.bfloat16)
    width_share = MODEL_WIDTH // tensor_count
    column_first = tensor_rank * width_share
    down_matrix = down_blocks.reshape(STORE_REQUESTS * 2 * ADAPTER_RANK, width_share)
    query_width = query_weight.shape[1]
    keyval_width = key_value_weight.shape[1]
    rows_piece = lax.all_gather(tokens, "tensor", axis=0, tiled=True)
    count = rows_piece.shape[0]
    plain_query = jnp.dot(rows_piece, query_weight, preferred_element_type=jnp.float32)
    plain_key_value = jnp.dot(rows_piece, key_value_weight, preferred_element_type=jnp.float32)
    features = lax.dynamic_slice_in_dim(rows_piece, column_first, width_share, 1)
    partial_low = lax.dot_general(
        features, down_matrix, (((1,), (1,)), ((), ())), preferred_element_type=jnp.float32
    )
    partial_low = jnp.sum(
        partial_low.reshape(count, STORE_REQUESTS, 2 * ADAPTER_RANK) * member_float[:, :, None],
        axis=1,
    )
    joined = jnp.concatenate([plain_query, plain_key_value, partial_low], axis=1)
    plain_query = joined[:, :query_width]
    plain_key_value = joined[:, query_width : query_width + keyval_width]
    low = lax.psum(joined[:, query_width + keyval_width :], "tensor").astype(jnp.bfloat16)
    token_query_update = (low[:, None, :ADAPTER_RANK] * member_half[:, :, None]).reshape(
        TOK_ST, STORE_REQUESTS * ADAPTER_RANK
    )
    token_key_value_update = (low[:, None, ADAPTER_RANK:] * member_half[:, :, None]).reshape(
        TOK_ST, STORE_REQUESTS * ADAPTER_RANK
    )
    query_update = jnp.dot(
        token_query_update,
        up_query_blocks.reshape(STORE_REQUESTS * ADAPTER_RANK, query_width),
        preferred_element_type=jnp.float32,
    )
    key_value_update = jnp.dot(
        token_key_value_update,
        up_keyval_blocks.reshape(STORE_REQUESTS * ADAPTER_RANK, keyval_width),
        preferred_element_type=jnp.float32,
    )
    query_unrotated = plain_query + adapter_scale * query_update
    key_value_unrotated = plain_key_value + adapter_scale * key_value_update
    positions = token_positions(segment_row)
    head_local = query_width // HEAD_SIZE
    query = rotary(query_unrotated.reshape(TOK_ST, head_local, HEAD_SIZE), positions).astype(
        jnp.bfloat16
    )
    pair_heads = keyval_width // HEAD_SIZE
    keyval_heads = key_value_unrotated.reshape(TOK_ST, pair_heads, HEAD_SIZE)
    holds_keys = tensor_rank % 2 == 0
    own_part = jnp.where(holds_keys, rotary(keyval_heads, positions), keyval_heads).astype(
        jnp.bfloat16
    )
    other_part = from_partner(own_part, "tensor", 0)
    keys = jnp.where(holds_keys, own_part, other_part)
    values = jnp.where(holds_keys, other_part, own_part)
    group_size = QUERY_HEADS // KEY_VALUE_HEADS
    kv_used = max(head_local // group_size, 1)
    per_kv = head_local // kv_used
    kv_first = tensor_rank * head_local // group_size - tensor_rank // 2 * pair_heads
    keys_used = lax.dynamic_slice_in_dim(keys, kv_first, kv_used, 1)
    values_used = lax.dynamic_slice_in_dim(values, kv_first, kv_used, 1)
    grouped = query.reshape(TOK_ST, kv_used, per_kv, HEAD_SIZE)
    scores = jnp.einsum(
        "tkgd,skd->kgts", grouped, keys_used, preferred_element_type=jnp.float32
    ) / math.sqrt(HEAD_SIZE)
    token_index = jnp.arange(TOK_ST, dtype=jnp.int32)
    allowed = (segment_row[:, None] == segment_row[None, :]) & (
        token_index[:, None] >= token_index[None, :]
    )
    scores = jnp.where(allowed, scores, -1e30)
    scores = scores - jnp.max(scores, axis=-1, keepdims=True)
    weights = jnp.exp(scores)
    weights = (weights / jnp.sum(weights, axis=-1, keepdims=True)).astype(jnp.bfloat16)
    mixed = jnp.einsum("kgts,skd->tkgd", weights, values_used, preferred_element_type=jnp.float32)
    return mixed.reshape(TOK_ST, query_width).astype(jnp.bfloat16)


def solution(mesh):
    return jax.shard_map(
        on_device,
        mesh=mesh,
        in_specs=(
            P(("groups", "store", "tensor"), None),
            P(None, "tensor"),
            P(None, "tensor"),
            P("store", None, "tensor"),
            P("store", None, "tensor"),
            P("store", None, "tensor"),
            P("groups"),
            P("groups", None),
            P(("groups", "store"), None),
        ),
        out_specs=P(("groups", "store"), "tensor"),
        check_vma=False,
    )
```

profile of v0, /device:TPU:0, one launch (start us, length us, event | category | flops | bytes accessed | tf_op | source)
XLA Modules:
  0.0 270.4 jit_solution(15919129932199313101)
XLA Ops:
  6.5 0.7 all-gather.2.cloned.1.call-update
  7.3 0.9 select_reduce_fusion.1
  8.2 0.1 convert_reduce_fusion.1
  8.3 1.4 convolution_convert_fusion.4
  9.7 0.0 copy-start.4
  9.7 0.7 copy.34
  10.5 4.2 %all-to-all-start.1 = ((bf16[4,64,512]{2,1,0:T(8,128)(2,1)}), bf16[4,64,512]{2,1,0:T(8,128)(2,1)S(1)}, u32[]{:S(2)}, u32[]{:S(2)}) async-start(bf16[4,64,512]{2,1,0:T(8,128)(2,1)} %copy.34), calls=%async_computation.1 | async-start | bytes 524288 | tf_op jit(solution)/shard_map/all_to_all | solution.py:80
  14.7 1.6 convolution_convert_fusion.3
  16.3 1.6 copy.40
  18.0 2.8 %all-to-all-done.1 = bf16[4,64,512]{2,1,0:T(8,128)(2,1)S(1)} async-done(((bf16[4,64,512]{2,1,0:T(8,128)(2,1)}), bf16[4,64,512]{2,1,0:T(8,128)(2,1)S(1)}, u32[]{:S(2)}, u32[]{:S(2)}) %all-to-all-start.1) | async-done | bytes 262176 | tf_op jit(solution)/shard_map/all_to_all | solution.py:80
  20.7 3.5 %all-to-all-start.2 = ((bf16[4,64,2048]{2,1,0:T(8,128)(2,1)}), bf16[4,64,2048]{2,1,0:T(8,128)(2,1)S(1)}, u32[]{:S(2)}, u32[]{:S(2)}) async-start(bf16[4,64,2048]{2,1,0:T(8,128)(2,1)} %copy.40), calls=%async_computation.2 | async-start | bytes 2097152 | tf_op jit(solution)/shard_map/all_to_all | solution.py:79
  24.3 0.1 convert_reduce_fusion
  24.4 0.2 reduce-window.8
  24.6 5.4 %convolution_convert_fusion = bf16[4,128,2048]{2,0,1:T(4,128)(2,1)S(1)} fusion(s32[4,8]{1,0:T(4,128)S(1)} %convert_reduce_fusion.1, bf16[1,8,128,2048]{3,2,1,0:T(8,128)(2,1)} %bitcast.125), kind=kOutput, calls=%fused_computation.14 | convolution fusion | flops 17825824 | bytes 6291584 | tf_op jit(solution)/shard_map/dot_general | solution.py:44
  30.0 2.5 copy.31
  32.5 6.2 %all-to-all-done.2 = bf16[4,64,2048]{2,1,0:T(8,128)(2,1)S(1)} async-done(((bf16[4,64,2048]{2,1,0:T(8,128)(2,1)}), bf16[4,64,2048]{2,1,0:T(8,128)(2,1)S(1)}, u32[]{:S(2)}, u32[]{:S(2)}) %all-to-all-start.2) | async-done | bytes 1048608 | tf_op jit(solution)/shard_map/all_to_all | solution.py:79
  38.7 1.0 copy-done.2
  39.7 3.8 %all-to-all-start = ((bf16[4,128,2048]{2,1,0:T(8,128)(2,1)}), bf16[4,128,2048]{2,1,0:T(8,128)(2,1)S(1)}, u32[]{:S(2)}, u32[]{:S(2)}) async-start(bf16[4,128,2048]{2,1,0:T(8,128)(2,1)} %copy.31), calls=%async_computation | async-start | bytes 4194304 | tf_op jit(solution)/shard_map/all_to_all | solution.py:78
  43.5 0.1 select_reduce_fusion
  43.6 0.2 fusion.31
  43.8 1.0 multiply_cosine_fusion
  44.8 0.4 convolution_convert_fusion.5
  45.2 3.3 %convolution_convert_fusion.2 = bf16[4,64,2048]{2,0,1:T(4,128)(2,1)} fusion(s32[4]{0:T(128)S(1)} %and_select_fusion, bf16[1,4,64,2048]{3,2,1,0:T(8,128)(2,1)} %bitcast.129), kind=kOutput, calls=%fused_computation.16 | convolution fusion | flops 4718608 | bytes 2097168 | tf_op jit(solution)/shard_map/dot_general | solution.py:44
  48.4 20.5 %all-to-all-done = bf16[4,128,2048]{2,1,0:T(8,128)(2,1)S(1)} async-done(((bf16[4,128,2048]{2,1,0:T(8,128)(2,1)}), bf16[4,128,2048]{2,1,0:T(8,128)(2,1)S(1)}, u32[]{:S(2)}, u32[]{:S(2)}) %all-to-all-start) | async-done | bytes 2097184 | tf_op jit(solution)/shard_map/all_to_all | solution.py:78
  68.9 3.1 %convolution_convert_fusion.1 = bf16[4,128,2048]{2,0,1:T(4,128)(2,1)} fusion(s32[4]{0:T(128)S(1)} %and_select_fusion, bf16[1,4,128,2048]{3,2,1,0:T(8,128)(2,1)S(1)} %bitcast.127), kind=kOutput, calls=%fused_computation.15 | convolution fusion | flops 9437200 | bytes 4194320 | tf_op jit(solution)/shard_map/dot_general | solution.py:44
  72.0 89.3 %all-gather.2.cloned.1.call-done = bf16[512,8192]{1,0:T(8,128)(2,1)} async-done(((bf16[128,8192]{1,0:T(8,128)(2,1)}), bf16[512,8192]{1,0:T(8,128)(2,1)}) %all-gather.2.cloned.1.call-update) | async-done | bytes 8388624 | tf_op jit(solution)/shard_map/all_gather | solution.py:97
  161.3 4.9 %fusion.24 = f32[512,128]{1,0:T(8,128)S(1)} fusion(bf16[4,128,2048]{2,0,1:T(4,128)(2,1)} %convolution_convert_fusion.1, bf16[512,8192]{1,0:T(8,128)(2,1)} %all-gather.2.cloned.1.call-done, s32[]{:T(128)S(6)} %select_n.62, f32[512,4]{0,1:T(4,128)S(1)} %get-tuple-element.14), kind=kOutput, calls=%fused_computation.31 | convolution fusion | flops 1074200576 | bytes 4464644 | tf_op jit(solution)/shard_map/dot_general | solution.py:102
  166.2 21.4 %all-reduce.1 = bf16[512,128]{1,0:T(8,128)(2,1)S(1)} all-reduce(f32[512,128]{1,0:T(8,128)S(1)} %fusion.24), channel_id=1, replica_groups=mesh['groups'=2,'tensor'=4,'store'=4] {'tensor'}, use_global_device_ids=true, to_apply=%region_3.4 | all-reduce | flops 65536 | bytes 393216 | tf_op jit(solution)/shard_map/psum | solution.py:112
  187.6 0.1 fusion.68
  187.7 0.1 copy.33
  187.8 9.5 %fusion.82 = f32[512,512]{0,1:T(8,128)S(1)} fusion(bf16[512,8192]{1,0:T(8,128)(2,1)} %all-gather.2.cloned.1.call-done, bf16[8192,512]{1,0:T(8,128)(2,1)} %param.11), kind=kOutput, calls=%fused_computation.106 | convolution fusion | flops 4294967296 | bytes 17825792 | tf_op jit(solution)/shard_map/dot_general | solution.py:100
  197.3 0.3 fusion.23
  197.6 0.3 copy.36
  197.9 0.1 copy.39
  198.1 0.4 multiply_subtract_fusion
  198.5 0.3 fusion.29
  198.8 0.1 collective-permute-start
  198.9 23.8 %fusion.83 = f32[512,2048]{1,0:T(8,128)S(1)} fusion(bf16[512,8192]{1,0:T(8,128)(2,1)} %all-gather.2.cloned.1.call-done, bf16[8192,2048]{1,0:T(8,128)(2,1)} %param.10), kind=kOutput, calls=%fused_computation.107 | convolution fusion | flops 17179869184 | bytes 46137344 | tf_op jit(solution)/shard_map/dot_general | solution.py:99
  222.8 1.7 fusion.7
  224.5 0.9 copy.58
  225.5 1.8 subtract_convert_fusion
  227.3 0.5 copy.42
  227.9 0.5 copy.43
  228.4 0.0 copy-start.3
  228.4 8.2 %fusion.8 = f32[2,512,512,8]{2,1,3,0:T(8,128)} fusion(bf16[512,2,8,64]{3,0,2,1:T(8,128)(2,1)S(1)} %bitcast.123, bf16[512,2,8,64]{3,0,2,1:T(8,128)(2,1)S(1)} %bitcast.122, pred[]{:T(512)S(6)} %eq.43, bf16[512,4,128]{2,0,1:T(8,128)(2,1)S(1)} %fusion.29, s32[]{:T(128)S(6)} %select_n.70, bf16[512,4,128]{2,0,1:T(8,128)(2,1)S(1)} %collective-permute-done), kind=kOutput, calls=%fused_computation.18 | convolution fusion | flops 1078067200 | bytes 21495812 | tf_op jit(solution)/shard_map/tkgd,skd->kgts/dot_general | solution.py:152
  236.6 17.2 %fusion.69 = (f32[2,8,512]{2,1,0:T(8,128)S(1)}, f32[2,8,512,512]{2,3,1,0:T(8,128)}) fusion(f32[2,512,512,8]{2,1,3,0:T(8,128)} %fusion.8, pred[512,512]{0,1:T(8,128)(4,1)S(1)} %fusion.31), kind=kOutput, calls=%fused_computation.93 | output fusion | flops 25166336 | bytes 33849344 | tf_op jit(solution)/shard_map/sub | solution.py:160
  253.8 7.3 %fusion.16 = bf16[2,128,8,512]{3,1,2,0:T(8,128)(2,1)S(1)} fusion(f32[2,8,512,512]{2,3,1,0:T(8,128)} %get-tuple-element.16, f32[2,8,512]{2,1,0:T(8,128)S(1)} %get-tuple-element.15, pred[]{:T(512)S(6)} %eq.43, bf16[512,4,128]{2,0,1:T(8,128)(2,1)S(1)} %fusion.29, s32[]{:T(128)S(6)} %select_n.70, bf16[512,4,128]{2,0,1:T(8,128)(2,1)} %copy-done.3), kind=kOutput, calls=%fused_computation.26 | convolution fusion | flops 1083310080 | bytes 19431428 | tf_op jit(solution)/shard_map/kgts,skd->tkgd/dot_general | solution.py:163
  261.2 2.4 copy.46
  (15 shorter events, 0.1 us)
Async XLA Ops:
  6.5 8.2 %copy-start = (bf16[8,64,2048]{2,1,0:T(8,128)(2,1)S(1)}, bf16[8,64,2048]{2,1,0:T(8,128)(2,1)}, u32[]{:S(2)}) copy-start(bf16[8,64,2048]{2,1,0:T(8,128)(2,1)} %param.13) | copy-start | bytes 6291460
  6.5 154.7 %all-gather.2.cloned.1.call-start = ((), (), s32[]{:S(2)}) async-start(), calls=%async_computation.3 | async-start | bytes 10485760 | tf_op jit(solution)/shard_map/all_gather | solution.py:97
  9.7 14.6 %copy-start.4 = (s32[1,512]{1,0:T(1,128)S(1)}, s32[1,512]{1,0:T(1,128)}, u32[]{:S(2)}) copy-start(s32[1,512]{1,0:T(1,128)} %param.17) | copy-start | bytes 6148
  10.5 10.2 %all-to-all-start.1 = ((bf16[4,64,512]{2,1,0:T(8,128)(2,1)}), bf16[4,64,512]{2,1,0:T(8,128)(2,1)S(1)}, u32[]{:S(2)}, u32[]{:S(2)}) async-start(bf16[4,64,512]{2,1,0:T(8,128)(2,1)} %copy.34), calls=%async_computation.1 | async-start | bytes 524288 | tf_op jit(solution)/shard_map/all_to_all | solution.py:80
  20.7 17.9 %all-to-all-start.2 = ((bf16[4,64,2048]{2,1,0:T(8,128)(2,1)}), bf16[4,64,2048]{2,1,0:T(8,128)(2,1)S(1)}, u32[]{:S(2)}, u32[]{:S(2)}) async-start(bf16[4,64,2048]{2,1,0:T(8,128)(2,1)} %copy.40), calls=%async_computation.2 | async-start | bytes 2097152 | tf_op jit(solution)/shard_map/all_to_all | solution.py:79
  38.7 1.0 copy-start.2
  39.7 29.3 %all-to-all-start = ((bf16[4,128,2048]{2,1,0:T(8,128)(2,1)}), bf16[4,128,2048]{2,1,0:T(8,128)(2,1)S(1)}, u32[]{:S(2)}, u32[]{:S(2)}) async-start(bf16[4,128,2048]{2,1,0:T(8,128)(2,1)} %copy.31), calls=%async_computation | async-start | bytes 4194304 | tf_op jit(solution)/shard_map/all_to_all | solution.py:78
  198.8 23.9 %copy-start.1 = (bf16[4,64,2048]{2,0,1:T(4,128)(2,1)S(1)}, bf16[4,64,2048]{2,0,1:T(4,128)(2,1)}, u32[]{:S(2)}) copy-start(bf16[4,64,2048]{2,0,1:T(4,128)(2,1)} %convolution_convert_fusion.2) | copy-start | bytes 3145732
  198.8 29.6 %collective-permute-start = (bf16[512,4,128]{2,0,1:T(8,128)(2,1)S(1)}, bf16[512,4,128]{2,0,1:T(8,128)(2,1)S(1)}, u32[]{:S(2)}, u32[]{:S(2)}) collective-permute-start(bf16[512,4,128]{2,0,1:T(8,128)(2,1)S(1)} %fusion.29), channel_id=1, source_target_pairs={{0,4},{4,0},{8,12},{12,8},{1,5},{5,1},{9,13},{13,9},{2,6},{6,2},{1... | collective-permute-start | bytes 1572872 | tf_op jit(solution)/shard_map/ppermute | solution.py:19
  228.4 8.2 %copy-start.3 = (bf16[512,4,128]{2,0,1:T(8,128)(2,1)}, bf16[512,4,128]{2,0,1:T(8,128)(2,1)S(1)}, u32[]{:S(2)}) copy-start(bf16[512,4,128]{2,0,1:T(8,128)(2,1)S(1)} %collective-permute-done) | copy-start | bytes 1572868
Sparse Core Ops, SparseCore 0:
  8.9 152.3 all-gather.1
where the time goes:
time: 271 us; the launch traced here: 270 us
  waiting for transfers between devices  119 us (44%)
  matrix products  71 us (26%)
  other arithmetic  22.4 us (8%)
  blocking collectives  21.4 us (8%)
  between operations  13.7 us (5%)
  starting transfers between devices  11.6 us (4%)
  local copies, waits for them, and re-layouts  10.9 us (4%)
    all_gather x1, waiting for transfers between devices, on_device(): rows_piece = lax.all_gather(tokens, 'tensor', axis=0, tiled=True)  89.3 us
    dot_general x1, matrix products, on_device(): jnp.dot(rows_piece, query_weight, preferred_element_type=jnp.float32)  23.8 us
    psum x1, blocking collectives, on_device(): lax.psum(joined[:, query_width + keyval_width:], 'tensor')  21.4 us
    all_to_all x1, waiting for transfers between devices, on_device(): lax.all_to_all(out_down, 'store', split_axis=0, concat_axis=0, tiled=True)  20.5 us
    sub x1, other arithmetic, on_device(): scores = scores - jnp.max(scores, axis=-1, keepdims=True)  17.2 us
    dot_general x6, matrix products, select_rows(): picked = jnp.dot(selector, flat, preferred_element_type=jnp.float32)  15.1 us
    dot_general x1, matrix products, on_device(): jnp.dot(rows_piece, key_value_weight, preferred_element_type=jnp.float32)  9.46 us
    dot_general x1, matrix products, on_device(): jnp.einsum('tkgd,skd->kgts', grouped, keys_used, preferred_element_type=j...  8.15 us
  transfers between devices with their start and end apart: 5, of which 4 were waited for; matrix products, arithmetic and copies ran while one was open for 19% of the time, Pallas kernels for 0%

commit v1 on v0

--- a/solution.py
+++ b/solution.py
@@ -94,7 +94,10 @@
     down_matrix = down_blocks.reshape(STORE_REQUESTS * 2 * ADAPTER_RANK, width_share)
     query_width = query_weight.shape[1]
     keyval_width = key_value_weight.shape[1]
-    rows_piece = lax.all_gather(tokens, "tensor", axis=0, tiled=True)
+    piece_out = lax.axis_size("tensor")
+    current_block = jnp.stack(piece_out * [tokens])
+    carry_in = lax.all_to_all(current_block, axis_name="tensor", split_axis=0, concat_axis=0)
+    rows_piece = jnp.concatenate(carry_in, axis=0)
     count = rows_piece.shape[0]
     plain_query = jnp.dot(rows_piece, query_weight, preferred_element_type=jnp.float32)
     plain_key_value = jnp.dot(rows_piece, key_value_weight, preferred_element_type=jnp.float32)

time: 271 us -> 362 us (1.34)
  waiting for transfers between devices: 119 us -> 186 us
  blocking collectives: 21.4 us -> 51.1 us
  between operations: 13.7 us -> 0.28 us
    all_to_all x1, waiting for transfers between devices: 20.5 us -> 175 us  [on_device(): lax.all_to_all(current_block, axis_name='tensor', split_axis=0, concat_ax...]
    all_gather x1 -> x0, waiting for transfers between devices: 89.3 us -> none  [on_device(): rows_piece = lax.all_gather(tokens, 'tensor', axis=0, tiled=True)]
    all_to_all x0 -> x1, blocking collectives: none -> 29.1 us  [on_device(): lax.all_to_all(out_down, 'store', split_axis=0, concat_axis=0, tiled=True)]
    another operation x2 -> x3, local copies, waits for them, and re-layouts: 1.08 us -> 5.49 us  [the longest x1 4.41 us: on_device(): current_block = jnp.stack(piece_out * [tokens])]
  transfers between devices with their start and end apart: 5 -> 4, of which waited for: 4 -> 4; matrix products, arithmetic and copies ran while one was open for 19% -> 7% of each run, Pallas kernels for 0% -> 0%
where the time goes in v1:
time: 362 us
  waiting for transfers between devices  186 us (51%)
  matrix products  73.2 us (20%)
  blocking collectives  51.1 us (14%)
  other arithmetic  23.1 us (6%)
  local copies, waits for them, and re-layouts  14.5 us (4%)
  starting transfers between devices  13.8 us (4%)
    all_to_all x1, waiting for transfers between devices, on_device(): lax.all_to_all(current_block, axis_name='tensor', split_axis=0, concat_ax...  175 us
    all_to_all x1, blocking collectives, on_device(): lax.all_to_all(out_down, 'store', split_axis=0, concat_axis=0, tiled=True)  29.1 us
    dot_general x1, matrix products, on_device(): jnp.dot(rows_piece, query_weight, preferred_element_type=jnp.float32)  24.8 us
    psum x1, blocking collectives, on_device(): lax.psum(joined[:, query_width + keyval_width:], 'tensor')  21.9 us
    sub x1, other arithmetic, on_device(): scores = scores - jnp.max(scores, axis=-1, keepdims=True)  17.2 us
    dot_general x6, matrix products, select_rows(): picked = jnp.dot(selector, flat, preferred_element_type=jnp.float32)  16.5 us
    dot_general x1, matrix products, on_device(): jnp.dot(rows_piece, key_value_weight, preferred_element_type=jnp.float32)  9.46 us
    dot_general x1, matrix products, on_device(): jnp.einsum('tkgd,skd->kgts', grouped, keys_used, preferred_element_type=j...  8.15 us
  transfers between devices with their start and end apart: 4, of which 4 were waited for; matrix products, arithmetic and copies ran while one was open for 7% of the time, Pallas kernels for 0%

profile of v1, /device:TPU:0, one launch (start us, length us, event | category | flops | bytes accessed | tf_op | source)
XLA Modules:
  0.0 361.7 jit_solution(13655176128828658042)
XLA Ops:
  0.0 0.9 select_reduce_fusion.1
  0.9 0.1 convert_reduce_fusion.1
  1.0 1.4 convolution_convert_fusion.4
  2.5 0.7 copy.34
  3.2 4.2 %all-to-all-start.2 = ((bf16[4,64,512]{2,1,0:T(8,128)(2,1)}), bf16[4,64,512]{2,1,0:T(8,128)(2,1)S(1)}, u32[]{:S(2)}, u32[]{:S(2)}) async-start(bf16[4,64,512]{2,1,0:T(8,128)(2,1)} %copy.34), calls=%async_computation.2 | async-start | bytes 524288 | tf_op jit(solution)/shard_map/all_to_all | solution.py:80
  7.4 3.2 convolution_convert_fusion.3
  10.6 1.5 copy.40
  12.2 1.3 all-to-all-done.2
  13.4 3.5 all-to-all-start.3
  17.0 5.3 %convolution_convert_fusion = bf16[4,128,2048]{2,0,1:T(4,128)(2,1)S(1)} fusion(s32[4,8]{1,0:T(4,128)S(1)} %convert_reduce_fusion.1, bf16[1,8,128,2048]{3,2,1,0:T(8,128)(2,1)} %bitcast.126), kind=kOutput, calls=%fused_computation.14 | convolution fusion | flops 17825824 | bytes 6291584 | tf_op jit(solution)/shard_map/dot_general | solution.py:44
  22.3 1.2 copy.31
  23.4 7.9 %all-to-all-done.3 = bf16[4,64,2048]{2,1,0:T(8,128)(2,1)S(1)} async-done(((bf16[4,64,2048]{2,1,0:T(8,128)(2,1)}), bf16[4,64,2048]{2,1,0:T(8,128)(2,1)S(1)}, u32[]{:S(2)}, u32[]{:S(2)}) %all-to-all-start.3) | async-done | bytes 1048608 | tf_op jit(solution)/shard_map/all_to_all | solution.py:79
  31.4 29.1 %all_to_all.20 = bf16[4,128,2048]{2,1,0:T(8,128)(2,1)} all-to-all(bf16[4,128,2048]{2,1,0:T(8,128)(2,1)S(1)} %copy.31), channel_id=1, replica_groups=mesh['groups'=2,'tensor'=4,'store'=4] {'store'}, dimensions={0} | all-to-all | bytes 4194304 | tf_op jit(solution)/shard_map/all_to_all | solution.py:78
  60.5 4.4 %stack.2 = bf16[4,128,8192]{2,1,0:T(8,128)(2,1)} broadcast(bf16[128,8192]{1,0:T(8,128)(2,1)S(1)} %copy-done.1), dimensions={1,2} | broadcast | bytes 10485760 | tf_op jit(solution)/shard_map/stack | solution.py:98
  64.9 6.0 %all-to-all-start = ((bf16[4,128,8192]{2,1,0:T(8,128)(2,1)}), bf16[4,128,8192]{2,1,0:T(8,128)(2,1)}, u32[]{:S(2)}, u32[]{:S(2)}) async-start(bf16[4,128,8192]{2,1,0:T(8,128)(2,1)} %stack.2), calls=%async_computation | async-start | bytes 16777216 | tf_op jit(solution)/shard_map/all_to_all | solution.py:99
  71.0 0.1 convert_reduce_fusion
  71.1 0.2 reduce-window.8
  71.3 0.1 select_reduce_fusion
  71.4 0.9 fusion.31
  72.3 1.0 multiply_cosine_fusion
  73.3 0.4 convolution_convert_fusion.5
  73.7 3.2 convolution_convert_fusion.2
  76.8 3.1 convolution_convert_fusion.1
  79.9 174.5 %all-to-all-done = bf16[4,128,8192]{2,1,0:T(8,128)(2,1)} async-done(((bf16[4,128,8192]{2,1,0:T(8,128)(2,1)}), bf16[4,128,8192]{2,1,0:T(8,128)(2,1)}, u32[]{:S(2)}, u32[]{:S(2)}) %all-to-all-start) | async-done | bytes 8388640 | tf_op jit(solution)/shard_map/all_to_all | solution.py:99
  254.5 4.9 %fusion.24 = f32[512,128]{1,0:T(8,128)S(1)} fusion(bf16[4,128,2048]{2,0,1:T(4,128)(2,1)} %convolution_convert_fusion.1, bf16[512,8192]{1,0:T(8,128)(2,1)} %bitcast, s32[]{:T(128)S(6)} %select_n.62, f32[512,4]{0,1:T(4,128)S(1)} %get-tuple-element.14), kind=kOutput, calls=%fused_computation.31 | convolution fusion | flops 1074200576 | bytes 4464644 | tf_op jit(solution)/shard_map/dot_general | solution.py:105
  259.4 21.9 %all-reduce.1 = bf16[512,128]{1,0:T(8,128)(2,1)S(1)} all-reduce(f32[512,128]{1,0:T(8,128)S(1)} %fusion.24), channel_id=1, replica_groups=mesh['groups'=2,'tensor'=4,'store'=4] {'tensor'}, use_global_device_ids=true, to_apply=%region_3.4 | all-reduce | flops 65536 | bytes 393216 | tf_op jit(solution)/shard_map/psum | solution.py:115
  281.4 0.1 fusion.68
  281.5 0.1 copy.33
  281.6 0.1 copy.39
  281.7 9.5 %fusion.82 = f32[512,512]{0,1:T(8,128)S(1)} fusion(bf16[512,8192]{1,0:T(8,128)(2,1)} %bitcast, bf16[8192,512]{1,0:T(8,128)(2,1)} %param.11), kind=kOutput, calls=%fused_computation.106 | convolution fusion | flops 4294967296 | bytes 17825792 | tf_op jit(solution)/shard_map/dot_general | solution.py:103
  291.1 24.8 %fusion.83 = f32[512,2048]{1,0:T(8,128)} fusion(bf16[512,8192]{1,0:T(8,128)(2,1)} %bitcast, bf16[8192,2048]{1,0:T(8,128)(2,1)} %param.10), kind=kOutput, calls=%fused_computation.107 | convolution fusion | flops 17179869184 | bytes 46137344 | tf_op jit(solution)/shard_map/dot_general | solution.py:102
  316.0 0.3 fusion.23
  316.3 0.3 copy.36
  316.7 0.4 multiply_subtract_fusion
  317.1 0.3 fusion.29
  317.4 0.1 collective-permute-start
  317.5 1.3 copy-done
  318.8 0.3 copy-done.3
  319.1 1.8 fusion.7
  320.9 0.9 copy.58
  321.8 1.8 subtract_convert_fusion
  323.7 0.5 copy.42
  324.2 0.5 copy.43
  324.8 1.9 collective-permute-done
  326.7 8.2 %fusion.8 = f32[2,512,512,8]{2,1,3,0:T(8,128)} fusion(bf16[512,2,8,64]{3,0,2,1:T(8,128)(2,1)S(1)} %bitcast.124, bf16[512,2,8,64]{3,0,2,1:T(8,128)(2,1)S(1)} %bitcast.123, pred[]{:T(512)S(6)} %eq.43, bf16[512,4,128]{2,0,1:T(8,128)(2,1)S(1)} %fusion.29, s32[]{:T(128)S(6)} %select_n.70, bf16[512,4,128]{2,0,1:T(8,128)(2,1)S(1)} %collective-permute-done), kind=kOutput, calls=%fused_computation.18 | convolution fusion | flops 1078067200 | bytes 21495812 | tf_op jit(solution)/shard_map/tkgd,skd->kgts/dot_general | solution.py:155
  334.8 17.2 %fusion.69 = (f32[2,8,512]{2,1,0:T(8,128)S(1)}, f32[2,8,512,512]{2,3,1,0:T(8,128)}) fusion(f32[2,512,512,8]{2,1,3,0:T(8,128)} %fusion.8, pred[512,512]{0,1:T(8,128)(4,1)S(1)} %copy-done.5), kind=kOutput, calls=%fused_computation.93 | output fusion | flops 25166336 | bytes 33849344 | tf_op jit(solution)/shard_map/sub | solution.py:163
  352.1 7.2 %fusion.16 = bf16[2,128,8,512]{3,1,2,0:T(8,128)(2,1)S(1)} fusion(f32[2,8,512,512]{2,3,1,0:T(8,128)} %get-tuple-element.16, f32[2,8,512]{2,1,0:T(8,128)S(1)} %get-tuple-element.15, pred[]{:T(512)S(6)} %eq.43, bf16[512,4,128]{2,0,1:T(8,128)(2,1)S(1)} %fusion.29, s32[]{:T(128)S(6)} %select_n.70, bf16[512,4,128]{2,0,1:T(8,128)(2,1)S(1)} %collective-permute-done), kind=kOutput, calls=%fused_computation.26 | convolution fusion | flops 1083310080 | bytes 19431428 | tf_op jit(solution)/shard_map/kgts,skd->tkgd/dot_general | solution.py:166
  359.3 2.4 copy.46
  (18 shorter events, 0.1 us)
Async XLA Ops:
  3.2 10.2 %all-to-all-start.2 = ((bf16[4,64,512]{2,1,0:T(8,128)(2,1)}), bf16[4,64,512]{2,1,0:T(8,128)(2,1)S(1)}, u32[]{:S(2)}, u32[]{:S(2)}) async-start(bf16[4,64,512]{2,1,0:T(8,128)(2,1)} %copy.34), calls=%async_computation.2 | async-start | bytes 524288 | tf_op jit(solution)/shard_map/all_to_all | solution.py:80
  13.4 17.9 %all-to-all-start.3 = ((bf16[4,64,2048]{2,1,0:T(8,128)(2,1)}), bf16[4,64,2048]{2,1,0:T(8,128)(2,1)S(1)}, u32[]{:S(2)}, u32[]{:S(2)}) async-start(bf16[4,64,2048]{2,1,0:T(8,128)(2,1)} %copy.40), calls=%async_computation.3 | async-start | bytes 2097152 | tf_op jit(solution)/shard_map/all_to_all | solution.py:79
  31.4 33.6 %copy-start.4 = (bf16[4,64,2048]{2,1,0:T(8,128)(2,1)}, bf16[4,64,2048]{2,1,0:T(8,128)(2,1)S(1)}, u32[]{:S(2)}) copy-start(bf16[4,64,2048]{2,1,0:T(8,128)(2,1)S(1)} %all-to-all-done.3) | copy-start | bytes 3145732
  31.4 29.2 %copy-start.1 = (bf16[128,8192]{1,0:T(8,128)(2,1)S(1)}, bf16[128,8192]{1,0:T(8,128)(2,1)}, u32[]{:S(2)}) copy-start(bf16[128,8192]{1,0:T(8,128)(2,1)} %param.9) | copy-start | bytes 6291460
  64.9 6.0 %copy-start.6 = (s32[1,512]{1,0:T(1,128)S(1)}, s32[1,512]{1,0:T(1,128)}, u32[]{:S(2)}) copy-start(s32[1,512]{1,0:T(1,128)} %param.17) | copy-start | bytes 6148
  64.9 11.9 %copy-start.2 = (bf16[4,128,2048]{2,1,0:T(8,128)(2,1)S(1)}, bf16[4,128,2048]{2,1,0:T(8,128)(2,1)}, u32[]{:S(2)}) copy-start(bf16[4,128,2048]{2,1,0:T(8,128)(2,1)} %all_to_all.20) | copy-start | bytes 6291460
  64.9 189.5 %all-to-all-start = ((bf16[4,128,8192]{2,1,0:T(8,128)(2,1)}), bf16[4,128,8192]{2,1,0:T(8,128)(2,1)}, u32[]{:S(2)}, u32[]{:S(2)}) async-start(bf16[4,128,8192]{2,1,0:T(8,128)(2,1)} %stack.2), calls=%async_computation | async-start | bytes 16777216 | tf_op jit(solution)/shard_map/all_to_all | solution.py:99
  316.7 2.2 copy-start
  316.7 2.5 copy-start.3
  317.4 9.2 %collective-permute-start = (bf16[512,4,128]{2,0,1:T(8,128)(2,1)S(1)}, bf16[512,4,128]{2,0,1:T(8,128)(2,1)S(1)}, u32[]{:S(2)}, u32[]{:S(2)}) collective-permute-start(bf16[512,4,128]{2,0,1:T(8,128)(2,1)S(1)} %fusion.29), channel_id=1, source_target_pairs={{0,4},{4,0},{8,12},{12,8},{1,5},{5,1},{9,13},{13,9},{2,6},{6,2},{1... | collective-permute-start | bytes 1572872 | tf_op jit(solution)/shard_map/ppermute | solution.py:19
  326.7 8.2 %copy-start.5 = (pred[512,512]{0,1:T(8,128)(4,1)S(1)}, pred[512,512]{0,1:T(8,128)(4,1)}, u32[]{:S(2)}) copy-start(pred[512,512]{0,1:T(8,128)(4,1)} %fusion.31) | copy-start | bytes 786436
